TPU v7x, 32 devices: a whole 2x2x4 slice. The times are simulated.
32 devices in a mesh: groups: 2 (over y), expert: 8 (over z, core), section: 2 (over x), tensor: 1.
Axes of the slice: x: 2, y: 2, z: 4, core: 2. Of those that a mesh axis runs over, the one named last changes fastest.
Arguments:
- opening_residual: bfloat16 [2, 2048, 2048], P('section', ('groups', 'expert'), 'tensor'), parts along dimension 1, may hold values from -12 to 12
- incoming_residual: bfloat16 [1, 2048, 2048], P(None, ('groups', 'expert'), 'tensor'), parts along dimension 1, may hold values from -12 to 12
- stored_summaries: bfloat16 [2, 2, 16, 768, 512], P(None, 'section', ('groups', 'expert')), parts along dimension 2, may hold values from -40 to 40
- stored_counts: int32 [3, 16], P(None, ('groups', 'expert')), parts along dimension 1, may hold values from 1 to 768, as said below
- picked_specialists: int32 [2, 2, 2048, 6], P(None, 'section', ('groups', 'expert')), parts along dimension 2, may hold values from 0 to 15, all different within a row; in each aligned block of 128 rows (0 to 127, 128 to 255, ..., all dimensions but the last counted through in order) at most 64 rows name the same one
- chooser_mixing_share: float32 [2, 2, 2048, 6], P(None, 'section', ('groups', 'expert')), parts along dimension 2, may hold values from 0.05 to 0.4
- mixing_scale_factor: float32 [2, 2048], P('section'), may hold values from 0.25 to 1.75
- asking_projection: bfloat16 [2, 2048, 1024], P('section', None, 'tensor'), may hold values from -0.125 to 0.125
- summary_lookup_factor: bfloat16 [2, 8, 128, 512], P('section', 'tensor'), may hold values from -0.5 to 0.5
- summary_content_factor: bfloat16 [2, 8, 512, 128], P('section', 'tensor'), may hold values from -0.25 to 0.25
- merging_projection: bfloat16 [2, 1024, 2048], P('section', 'tensor'), may hold values from -0.1875 to 0.1875
- compress_projection: bfloat16 [2, 2048, 512], P('section', None, 'tensor'), may hold values from -0.125 to 0.125
- summary_scale_factor: float32 [2, 512], P('section'), may hold values from 0.25 to 1.75
- specialist_scale_factor: float32 [2, 2048], P('section', 'tensor'), may hold values from 0.25 to 1.75
- specialist_switch_factor: bfloat16 [2, 16, 2048, 704], P('section', 'expert', None, 'tensor'), may hold values from -0.125 to 0.125
- specialist_widen_factor: bfloat16 [2, 16, 2048, 704], P('section', 'expert', None, 'tensor'), may hold values from -0.125 to 0.125
- specialist_contract_factor: bfloat16 [2, 16, 704, 2048], P('section', 'expert', 'tensor'), may hold values from -0.21875 to 0.21875
Outputs:
- results: bfloat16 [2, 2, 2048, 2048], P(None, 'section', ('groups', 'expert'), 'tensor'), parts along dimension 2
There are 2 independent parts, one for each index of `groups`. A program takes and returns all parts, laid end to end along the dimension named above; an argument that names none is the same for every part. Nothing has to cross between parts.
Inputs may be any that keep to these rules, and one draw needn't show every extreme that they name: `picked_specialists`: in each aligned block of 128 rows (one sequence) no expert is chosen by more than 64 rows, a bound that some block reaches; each row names 6 different experts. `stored_counts`: in every microbatch some sequence has exactly 768 cached tokens.
All inputs are finite; a program needn't handle non-finite values.
Results may differ from a plain program's by a relative error of at most 0.04.
Values may be sent and summed in bfloat16 or wider, within the bound.
A program may use at most 128 MiB of HBM per device.

v0:
```python
import jax
import jax.numpy as jnp
from jax import lax
from jax.sharding import PartitionSpec as P

CAP = 64
RETURN_CHUNKS = 2
epsilon = 1e-06


def shifted(value, axis, steps):
    count = lax.axis_size(axis)
    initial, last = (max(0, -steps), min(count, count - steps))
    return lax.ppermute(value, axis, [(source, source + steps) for source in range(initial, last)])


def row_norm(values, gain_row):
    return (
        values * lax.rsqrt(jnp.mean(values * values, axis=-1, keepdims=True) + epsilon) * gain_row
    )


def attend(q_lat, cache_rows, new_rows, length, score_scale):
    piece_list = q_lat.shape[0]
    context = cache_rows.shape[0]
    key_rows = jnp.concatenate([cache_rows, new_rows], axis=0)
    scores = (
        jnp.einsum("thl,kl->thk", q_lat, key_rows, preferred_element_type=jnp.float32) * score_scale
    )
    position = lax.broadcasted_iota(jnp.int32, (piece_list, context + piece_list), 1)
    query_pos = lax.broadcasted_iota(jnp.int32, (piece_list, context + piece_list), 0)
    visible = jnp.where(position < context, position < length, position - context <= query_pos)
    scores = jnp.where(visible[:, None, :], scores, -jnp.inf)
    row_max = jnp.max(scores, axis=-1, keepdims=True)
    expd = jnp.where(visible[:, None, :], jnp.exp(scores - row_max), 0.0)
    attention = (expd / jnp.sum(expd, axis=-1, keepdims=True)).astype(jnp.bfloat16)
    return jnp.einsum(
        "thk,kl->thl", attention, key_rows, preferred_element_type=jnp.float32
    ).astype(jnp.bfloat16)


def shards(
    opening_residual,
    incoming_residual,
    stored_summaries,
    stored_counts,
    picked_specialists,
    chooser_mixing_share,
    mixing_scale_factor,
    asking_projection,
    summary_lookup_factor,
    summary_content_factor,
    merging_projection,
    compress_projection,
    summary_scale_factor,
    specialist_scale_factor,
    specialist_switch_factor,
    specialist_widen_factor,
    specialist_contract_factor,
):
    segment_ordinal = lax.axis_index("section")
    section_count = lax.axis_size("section")
    sources = lax.axis_size("expert")
    tick_count = stored_summaries.shape[0]
    piece_list = opening_residual.shape[1]
    inner_feature_midcount = opening_residual.shape[2]
    full_width = mixing_scale_factor.shape[1]
    local_heads = summary_lookup_factor.shape[1]
    head_size = summary_lookup_factor.shape[2]
    top_count = picked_specialists.shape[3]
    expert_local = specialist_switch_factor.shape[1]
    score_scale = head_size ** (-0.5)
    expert_ids = lax.broadcasted_iota(jnp.int32, (1, 1, 1, expert_local * sources), 3)
    shares_dense = jnp.sum(
        jnp.where(
            picked_specialists[:, 0][..., None] == expert_ids,
            chooser_mixing_share[:, 0][..., None],
            0.0,
        ),
        axis=2,
    )
    shares_all = lax.all_gather(jnp.swapaxes(shares_dense, 1, 2), "expert", axis=1, tiled=False)
    mine = lax.dynamic_slice_in_dim(
        shares_all, lax.axis_index("expert") * expert_local, expert_local, axis=2
    )
    chosen = mine > 0.0
    earlier_or_same = (
        lax.broadcasted_iota(jnp.int32, (piece_list, piece_list), 0)
        <= lax.broadcasted_iota(jnp.int32, (piece_list, piece_list), 1)
    ).astype(jnp.bfloat16)
    rank = jnp.einsum(
        "tjer,rq->tjeq",
        chosen.astype(jnp.bfloat16),
        earlier_or_same,
        preferred_element_type=jnp.float32,
    ).astype(jnp.int32)
    slots = lax.broadcasted_iota(jnp.int32, (1, 1, 1, CAP, 1), 3) + 1
    at_slot = (rank[..., None, :] == slots) & chosen[..., None, :]
    placed = at_slot.astype(jnp.bfloat16)
    slot_share = jnp.sum(jnp.where(at_slot, mine[..., None, :], 0.0), axis=-1)
    outputs = []
    present_carry = opening_residual[0]
    section_out = present_carry
    for step_index in range(tick_count):
        if step_index > 0:
            handed = shifted(section_out, "section", 1)
            present_carry = jnp.where(
                segment_ordinal == 0, incoming_residual[step_index - 1], handed
            )
        micro_index = step_index - segment_ordinal + section_count - 1
        length = lax.dynamic_index_in_dim(stored_counts[:, 0], micro_index, 0, keepdims=False)
        full_rows = lax.all_gather(present_carry, "tensor", axis=1, tiled=True)
        normed = row_norm(full_rows.astype(jnp.float32), mixing_scale_factor[0]).astype(
            jnp.bfloat16
        )
        queries = jnp.dot(normed, asking_projection[0], preferred_element_type=jnp.float32).astype(
            jnp.bfloat16
        )
        queries = queries.reshape(piece_list, local_heads, head_size)
        q_lat = jnp.einsum(
            "thd,hdl->thl", queries, summary_lookup_factor[0], preferred_element_type=jnp.float32
        ).astype(jnp.bfloat16)
        latent_part = jnp.dot(normed, compress_projection[0], preferred_element_type=jnp.float32)
        latent_raw = lax.all_gather(
            latent_part.astype(jnp.bfloat16), "tensor", axis=1, tiled=True
        ).astype(latent_part.dtype)
        new_latent = row_norm(latent_raw, summary_scale_factor[0]).astype(jnp.bfloat16)
        o_lat = attend(q_lat, stored_summaries[step_index, 0, 0], new_latent, length, score_scale)
        heads_out = jnp.einsum(
            "thl,hld->thd", o_lat, summary_content_factor[0], preferred_element_type=jnp.float32
        ).astype(jnp.bfloat16)
        heads_out = heads_out.reshape(piece_list, local_heads * head_size)
        head_terms = jnp.dot(heads_out, merging_projection[0], preferred_element_type=jnp.float32)
        residual = present_carry.astype(jnp.float32) + lax.psum_scatter(
            head_terms.astype(jnp.bfloat16), "tensor", scatter_dimension=1, tiled=True
        ).astype(jnp.float32)
        squares = lax.psum(jnp.sum(residual * residual, axis=1), "tensor")
        moe_input = (
            residual
            * lax.rsqrt(squares / full_width + epsilon)[:, None]
            * specialist_scale_factor[0]
        ).astype(jnp.bfloat16)
        whole_rows = lax.all_gather(moe_input, "tensor", axis=1, tiled=True)
        place = placed[step_index]
        share = slot_share[step_index]
        all_rows = lax.all_gather(whole_rows, "expert", axis=0, tiled=True)
        all_rows = all_rows.reshape(sources, piece_list, full_width)
        hidden_list = []
        for e in range(expert_local):
            rows_in = jnp.einsum(
                "jsr,jrd->jsd", place[:, e], all_rows, preferred_element_type=jnp.float32
            ).astype(jnp.bfloat16)
            rows_in = rows_in.reshape(sources * CAP, full_width)
            gate_values = jnp.dot(
                rows_in, specialist_switch_factor[0, e], preferred_element_type=jnp.float32
            )
            up_values = jnp.dot(
                rows_in, specialist_widen_factor[0, e], preferred_element_type=jnp.float32
            )
            hidden_list.append(
                (jax.nn.silu(gate_values) * up_values * share[:, e].reshape(-1, 1)).astype(
                    jnp.bfloat16
                )
            )
        chunk = full_width // RETURN_CHUNKS
        routed_list = []
        for c in range(RETURN_CHUNKS):
            total = None
            for e in range(expert_local):
                down = jnp.dot(
                    hidden_list[e],
                    specialist_contract_factor[0, e][:, c * chunk : (c + 1) * chunk],
                    preferred_element_type=jnp.float32,
                ).astype(jnp.bfloat16)
                term = jnp.einsum(
                    "jsr,jsd->jrd",
                    place[:, e],
                    down.reshape(sources, CAP, chunk),
                    preferred_element_type=jnp.float32,
                )
                total = term if total is None else total + term
            total = total.astype(jnp.bfloat16).reshape(sources * piece_list, chunk)
            routed_list.append(lax.psum_scatter(total, "expert", scatter_dimension=0, tiled=True))
        routed = jnp.concatenate(routed_list, axis=1)
        routed = lax.psum_scatter(routed, "tensor", scatter_dimension=1, tiled=True).astype(
            jnp.float32
        )
        section_out = (residual + routed).astype(jnp.bfloat16)
        outputs.append(section_out)
    return jnp.stack(outputs)[:, None]


def solution(mesh):
    in_specs = (
        P("section", ("groups", "expert"), "tensor"),
        P(None, ("groups", "expert"), "tensor"),
        P(None, "section", ("groups", "expert"), None, None),
        P(None, ("groups", "expert")),
        P(None, "section", ("groups", "expert"), None),
        P(None, "section", ("groups", "expert"), None),
        P("section", None),
        P("section", None, "tensor"),
        P("section", "tensor", None, None),
        P("section", "tensor", None, None),
        P("section", "tensor", None),
        P("section", None, "tensor"),
        P("section", None),
        P("section", "tensor"),
        P("section", "expert", None, "tensor"),
        P("section", "expert", None, "tensor"),
        P("section", "expert", "tensor", None),
    )
    out_specs = P(None, "section", ("groups", "expert"), "tensor")
    return jax.shard_map(shards, mesh=mesh, in_specs=in_specs, out_specs=out_specs, check_vma=False)
```

profile of v0, /device:TPU:0, one launch (start us, length us, event | category | flops | bytes accessed | tf_op | source)
XLA Modules:
  0.0 368.0 jit_solution(13593333180121278280)
XLA Ops:
  11.4 3.0 fusion.130
  20.1 4.5 %fusion.105 = f32[128,8,896]{2,0,1:T(8,128)} fusion(bf16[1,8,128,512]{3,2,1,0:T(8,128)(2,1)S(1)} %copy-done.7, bf16[128,512]{1,0:T(8,128)(2,1)S(1)} %multiply_convert_fusion.3, bf16[768,512]{1,0:T(8,128)(2,1)} %get-tuple-element.10, bf16[16,8,8,128]{3,2,1,0:T(8,128)(2,1)S(1)} %fusion.130), kind=kOutput, calls=%fused_computation.97 | convolution fusion | flops 1076101120 | bytes 5898240 | tf_op jit(solution)/shard_map/thl,kl->thk/dot_general | solution.py:28
  24.6 6.7 %fusion.191 = (f32[128,8]{0,1:T(8,128)S(1)}, f32[128,8,896]{2,0,1:T(8,128)}) fusion(f32[128,8,896]{2,0,1:T(8,128)} %fusion.105, pred[128,896]{1,0:T(8,128)(4,1)} %get-tuple-element.20), kind=kOutput, calls=%fused_computation.204 | output fusion | flops 6423423 | bytes 7458816 | tf_op jit(solution)/shard_map/sub | solution.py:35
  31.3 3.9 %fusion.126 = bf16[8,128,128]{1,2,0:T(8,128)(2,1)S(1)} fusion(f32[128,8,896]{2,0,1:T(8,128)} %get-tuple-element.26, f32[128,8]{0,1:T(8,128)S(1)} %get-tuple-element.25, bf16[1,8,512,128]{3,2,1,0:T(8,128)(2,1)} %param.26, bf16[128,512]{1,0:T(8,128)(2,1)S(1)} %multiply_convert_fusion.3, bf16[768,512]{1,0:T(8,128)(2,1)S(1)} %copy-done.10), kind=kOutput, calls=%fused_computation.116 | convolution fusion | flops 1078067200 | bytes 5902336 | tf_op jit(solution)/shard_map/thl,hld->thd/dot_general | solution.py:129
  35.3 3.1 multiply_reduce_fusion.1
  39.6 16.3 %all-gather = f32[2,128,128]{2,1,0:T(8,128)S(1)} all-gather(f32[2,16,128]{2,1,0:T(8,128)S(1)} %bitcast.305), channel_id=2, replica_groups=mesh['groups'=2,'expert'=8,'section'=2,'tensor'=1] {'expert'}, dimensions={1}, use_global_device_ids=true | all-gather | bytes 147456 | tf_op jit(solution)/shard_map/all_gather | solution.py:82
  57.6 6.3 %slice_bitcast_fusion = (bf16[704,2048]{1,0:T(8,128)(2,1)}, bf16[704,2048]{1,0:T(8,128)(2,1)}) fusion(bf16[1,2,704,2048]{3,2,1,0:T(8,128)(2,1)} %param.33), kind=kLoop, calls=%fused_computation.40 | loop fusion | bytes 11534336 | tf_op jit(solution)/shard_map/squeeze | solution.py:172
  64.0 25.8 %all-gather.4.cloned.1.call-done = bf16[1024,2048]{1,0:T(8,128)(2,1)} async-done(((bf16[128,2048]{1,0:T(8,128)(2,1)}), bf16[1024,2048]{1,0:T(8,128)(2,1)}) %all-gather.4.cloned.1.call-update) | async-done | bytes 4194320 | tf_op jit(solution)/shard_map/all_gather | solution.py:146
  89.8 3.0 convolution_convert_fusion.2
  93.9 3.9 %fusion.16 = f32[512,704]{0,1:T(8,128)S(1)} fusion(bf16[512,2048]{1,0:T(8,128)(2,1)S(1)} %bitcast.286, bf16[1,2,2048,704]{2,3,1,0:T(8,128)(2,1)} %param.31), kind=kOutput, calls=%fused_computation.30 | convolution fusion | flops 1476395008 | bytes 6422528 | tf_op jit(solution)/shard_map/dot_general | solution.py:154
  115.4 27.9 %reduce-scatter.5.cloned.1.call-done = bf16[128,1024]{1,0:T(8,128)(2,1)} async-done(((bf16[1024,1024]{1,0:T(8,128)(2,1)}), bf16[128,1024]{1,0:T(8,128)(2,1)}) %reduce-scatter.5.cloned.1.call-update) | async-done | bytes 262160 | tf_op jit(solution)/shard_map/reduce_scatter | solution.py:183
  143.3 36.7 %reduce-scatter.7.cloned.1.call-done = bf16[128,1024]{1,0:T(8,128)(2,1)} async-done(((bf16[1024,1024]{1,0:T(8,128)(2,1)}), bf16[128,1024]{1,0:T(8,128)(2,1)}) %reduce-scatter.7.cloned.1.call-update) | async-done | bytes 262160 | tf_op jit(solution)/shard_map/reduce_scatter | solution.py:183
  182.0 3.4 collective-permute-start
  185.4 8.5 %collective-permute-done = bf16[128,2048]{1,0:T(8,128)(2,1)S(1)} collective-permute-done((bf16[128,2048]{1,0:T(8,128)(2,1)}, bf16[128,2048]{1,0:T(8,128)(2,1)S(1)}, u32[]{:S(2)}, u32[]{:S(2)}) %collective-permute-start) | collective-permute-done | bytes 524320 | tf_op jit(solution)/shard_map/ppermute | solution.py:14
  195.3 3.2 fusion.127
  199.7 4.5 %fusion.107 = f32[128,8,896]{2,0,1:T(8,128)} fusion(bf16[1,8,128,512]{3,2,1,0:T(8,128)(2,1)S(1)} %copy-done.8, bf16[128,512]{1,0:T(8,128)(2,1)S(1)} %multiply_convert_fusion.2, bf16[768,512]{1,0:T(8,128)(2,1)} %get-tuple-element.9, bf16[16,8,8,128]{3,2,1,0:T(8,128)(2,1)S(1)} %fusion.127), kind=kOutput, calls=%fused_computation.99 | convolution fusion | flops 1076101120 | bytes 5898240 | tf_op jit(solution)/shard_map/thl,kl->thk/dot_general | solution.py:28
  204.2 6.7 %fusion.192 = (f32[128,8]{0,1:T(8,128)S(1)}, f32[128,8,896]{2,0,1:T(8,128)}) fusion(f32[128,8,896]{2,0,1:T(8,128)} %fusion.107, pred[128,896]{1,0:T(8,128)(4,1)S(1)} %copy-done.18), kind=kOutput, calls=%fused_computation.205 | output fusion | flops 6423423 | bytes 7458816 | tf_op jit(solution)/shard_map/sub | solution.py:35
  211.0 3.7 %fusion.125 = bf16[8,128,128]{1,2,0:T(8,128)(2,1)S(1)} fusion(f32[128,8,896]{2,0,1:T(8,128)} %get-tuple-element.32, f32[128,8]{0,1:T(8,128)S(1)} %get-tuple-element.31, bf16[1,8,512,128]{3,2,1,0:T(8,128)(2,1)S(1)} %copy-done.28, bf16[128,512]{1,0:T(8,128)(2,1)S(1)} %multiply_convert_fusion.2, bf16[768,512]{1,0:T(8,128)(2,1)S(1)} %copy-done.9), kind=kOutput, calls=%fused_computation.115 | convolution fusion | flops 1078067200 | bytes 5902336 | tf_op jit(solution)/shard_map/thl,hld->thd/dot_general | solution.py:129
  214.7 3.0 multiply_reduce_fusion
  219.1 48.1 %all-gather.6.cloned.1.call-done = bf16[1024,2048]{1,0:T(8,128)(2,1)} async-done(((bf16[128,2048]{1,0:T(8,128)(2,1)}), bf16[1024,2048]{1,0:T(8,128)(2,1)}) %all-gather.6.cloned.1.call-update) | async-done | bytes 4194320 | tf_op jit(solution)/shard_map/all_gather | solution.py:146
  267.2 3.0 convolution_convert_fusion
  271.4 3.6 fusion.14
  292.6 28.2 %reduce-scatter.9.cloned.1.call-done = bf16[128,1024]{1,0:T(8,128)(2,1)} async-done(((bf16[1024,1024]{1,0:T(8,128)(2,1)}), bf16[128,1024]{1,0:T(8,128)(2,1)}) %reduce-scatter.9.cloned.1.call-update) | async-done | bytes 262160 | tf_op jit(solution)/shard_map/reduce_scatter | solution.py:183
  320.8 36.9 %reduce-scatter.11.cloned.1.call-done = bf16[128,1024]{1,0:T(8,128)(2,1)} async-done(((bf16[1024,1024]{1,0:T(8,128)(2,1)}), bf16[128,1024]{1,0:T(8,128)(2,1)}) %reduce-scatter.11.cloned.1.call-update) | async-done | bytes 262160 | tf_op jit(solution)/shard_map/reduce_scatter | solution.py:183
  (170 shorter events, 59.2 us)
Async XLA Ops:
  6.5 4.8 %copy-start.4 = (bf16[1,128,2048]{2,1,0:T(8,128)(2,1)S(1)}, bf16[1,128,2048]{2,1,0:T(8,128)(2,1)}, u32[]{:S(2)}) copy-start(bf16[1,128,2048]{2,1,0:T(8,128)(2,1)} %param.17) | copy-start | bytes 1572868
  6.5 4.8 %copy-start.19 = (f32[1,2048]{1,0:T(1,128)S(1)}, f32[1,2048]{1,0:T(1,128)}, u32[]{:S(2)}) copy-start(f32[1,2048]{1,0:T(1,128)} %param.23) | copy-start | bytes 24580
  6.5 83.2 %all-gather.4.cloned.1.call-start = ((), (), s32[]{:S(2)}) async-start(), calls=%async_computation.4 | async-start | bytes 4718592 | tf_op jit(solution)/shard_map/all_gather | solution.py:146
  11.3 4.3 %copy-start.27 = (s32[3,1]{0,1:T(1,128)S(1)}, s32[3,1]{0,1:T(1,128)}, u32[]{:S(2)}) copy-start(s32[3,1]{0,1:T(1,128)} %param.20) | copy-start | bytes 40
  11.3 6.1 %copy-start.23 = (f32[1,512]{1,0:T(1,128)S(1)}, f32[1,512]{1,0:T(1,128)}, u32[]{:S(2)}) copy-start(f32[1,512]{1,0:T(1,128)} %param.29) | copy-start | bytes 6148
  14.3 5.7 %copy-start.7 = (bf16[1,8,128,512]{3,2,1,0:T(8,128)(2,1)S(1)}, bf16[1,8,128,512]{3,2,1,0:T(8,128)(2,1)}, u32[]{:S(2)}) copy-start(bf16[1,8,128,512]{3,2,1,0:T(8,128)(2,1)} %param.25) | copy-start | bytes 3145732
  24.6 6.7 %copy-start.10 = (bf16[768,512]{1,0:T(8,128)(2,1)S(1)}, bf16[768,512]{1,0:T(8,128)(2,1)}, u32[]{:S(2)}) copy-start(bf16[768,512]{1,0:T(8,128)(2,1)} %get-tuple-element.10) | copy-start | bytes 2359300
  39.5 103.8 %reduce-scatter.5.cloned.1.call-start = ((), (), s32[]{:S(2)}) async-start(), calls=%async_computation.5 | async-start | bytes 2359296 | tf_op jit(solution)/shard_map/reduce_scatter | solution.py:183
  93.2 4.6 %slice-start = ((s8[5767168]{0:T(1024)(128)(4,1)}), s8[4194304]{0:T(1024)(128)(4,1)S(1)}, s32[]{:S(2)}) async-start(s8[5767168]{0:T(1024)(128)(4,1)} %bitcast.316), calls=%async_computation.10 | async-start | bytes 8388608
  93.9 5.6 %slice-start.4 = ((s8[5767168]{0:T(1024)(128)(4,1)}), s8[4194304]{0:T(1024)(128)(4,1)S(1)}, s32[]{:S(2)}) async-start(s8[5767168]{0:T(1024)(128)(4,1)} %bitcast.320), calls=%async_computation.14 | async-start | bytes 8388608
  108.6 71.4 %reduce-scatter.7.cloned.1.call-start = ((), (), s32[]{:S(2)}) async-start(), calls=%async_computation.6 | async-start | bytes 2359296 | tf_op jit(solution)/shard_map/reduce_scatter | solution.py:183
  115.3 151.9 %all-gather.6.cloned.1.call-start = ((), (), s32[]{:S(2)}) async-start(), calls=%async_computation.7 | async-start | bytes 4718592 | tf_op jit(solution)/shard_map/all_gather | solution.py:146
  182.0 12.0 %collective-permute-start = (bf16[128,2048]{1,0:T(8,128)(2,1)}, bf16[128,2048]{1,0:T(8,128)(2,1)S(1)}, u32[]{:S(2)}, u32[]{:S(2)}) collective-permute-start(bf16[128,2048]{1,0:T(8,128)(2,1)} %add_convert_fusion.5), channel_id=1, source_target_pairs={{0,1},{2,3},{4,5},{6,7},{8,9},{10,11},{12,13},{14,15},{16,17},{18,... | collective-permute-start | bytes 1572872 | tf_op jit(solution)/shard_map/ppermute | solution.py:14
  199.7 4.5 %copy-start.18 = (pred[128,896]{1,0:T(8,128)(4,1)S(1)}, pred[128,896]{1,0:T(8,128)(4,1)}, u32[]{:S(2)}) copy-start(pred[128,896]{1,0:T(8,128)(4,1)} %get-tuple-element.19) | copy-start | bytes 344068
  204.2 6.8 %copy-start.9 = (bf16[768,512]{1,0:T(8,128)(2,1)S(1)}, bf16[768,512]{1,0:T(8,128)(2,1)}, u32[]{:S(2)}) copy-start(bf16[768,512]{1,0:T(8,128)(2,1)} %get-tuple-element.9) | copy-start | bytes 2359300
  204.2 6.8 %copy-start.28 = (bf16[1,8,512,128]{3,2,1,0:T(8,128)(2,1)S(1)}, bf16[1,8,512,128]{3,2,1,0:T(8,128)(2,1)}, u32[]{:S(2)}) copy-start(bf16[1,8,512,128]{3,2,1,0:T(8,128)(2,1)} %param.26) | copy-start | bytes 3145732
  214.7 4.3 %copy-start.22 = (f32[8,1,64]{2,0,1:T(8,128)S(1)}, f32[8,1,64]{2,0,1:T(8,128)}, u32[]{:S(2)}) copy-start(f32[8,1,64]{2,0,1:T(8,128)} %get-tuple-element.15) | copy-start | bytes 6148
  214.7 4.4 %copy-start.21 = (f32[8,1,64]{2,0,1:T(8,128)S(1)}, f32[8,1,64]{2,0,1:T(8,128)}, u32[]{:S(2)}) copy-start(f32[8,1,64]{2,0,1:T(8,128)} %get-tuple-element.16) | copy-start | bytes 6148
  218.7 102.1 %reduce-scatter.9.cloned.1.call-start = ((), (), s32[]{:S(2)}) async-start(), calls=%async_computation.8 | async-start | bytes 2359296 | tf_op jit(solution)/shard_map/reduce_scatter | solution.py:183
  267.2 7.8 %slice-start.6 = ((s8[5767168]{0:T(1024)(128)(4,1)}), s8[4194304]{0:T(1024)(128)(4,1)S(1)}, s32[]{:S(2)}) async-start(s8[5767168]{0:T(1024)(128)(4,1)} %bitcast.322), calls=%async_computation.16 | async-start | bytes 8388608
  270.7 4.4 %slice-start.7 = ((s8[5767168]{0:T(1024)(128)(4,1)}), s8[1572864]{0:T(1024)(128)(4,1)S(1)}, s32[]{:S(2)}) async-start(s8[5767168]{0:T(1024)(128)(4,1)} %bitcast.322), calls=%async_computation.17 | async-start | bytes 3145728
  271.4 6.6 %slice-start.2 = ((s8[5767168]{0:T(1024)(128)(4,1)}), s8[4194304]{0:T(1024)(128)(4,1)S(1)}, s32[]{:S(2)}) async-start(s8[5767168]{0:T(1024)(128)(4,1)} %bitcast.318), calls=%async_computation.12 | async-start | bytes 8388608
  285.8 71.9 %reduce-scatter.11.cloned.1.call-start = ((), (), s32[]{:S(2)}) async-start(), calls=%async_computation.9 | async-start | bytes 2359296 | tf_op jit(solution)/shard_map/reduce_scatter | solution.py:183
  292.5 68.4 %copy-start.1 = (bf16[1,2048,512]{2,1,0:T(8,128)(2,1)S(1)}, bf16[1,2048,512]{2,1,0:T(8,128)(2,1)}, u32[]{:S(2)}) copy-start(bf16[1,2048,512]{2,1,0:T(8,128)(2,1)} %param.28) | copy-start | bytes 6291460
  (27 other events, 70.2 us)
Sparse Core Ops, SparseCore 0:
  39.6 50.1 all-gather.3
  108.7 34.5 reduce-scatter.4
  145.6 34.3 reduce-scatter.6
  218.8 48.3 all-gather.5
  285.9 34.8 reduce-scatter.8
  323.0 34.6 reduce-scatter.10
where the time goes:
time: 374 us; the launch traced here: 368 us
  waiting for transfers between devices  212 us (57%)
  matrix products  81 us (22%)
  other arithmetic  29.1 us (8%)
  blocking collectives  16.3 us (4%)
  between operations  14.6 us (4%)
  local copies, waits for them, and re-layouts  10.7 us (3%)
  starting transfers between devices  4.1 us (1%)
    reduce_scatter x4, waiting for transfers between devices, shards(): lax.psum_scatter(total, 'expert', scatter_dimension=0, tiled=True)  130 us
    all_gather x2, waiting for transfers between devices, shards(): all_rows = lax.all_gather(whole_rows, 'expert', axis=0, tiled=True)  73.9 us
    all_gather x1, blocking collectives, shards(): lax.all_gather(jnp.swapaxes(shares_dense, 1, 2), 'expert', axis=1, tiled=...  16.3 us
    sub x2, other arithmetic, attend(): expd = jnp.where(visible[:, None, :], jnp.exp(scores - row_max), 0.0)  13.5 us
    dot_general x8, matrix products, shards(): jnp.einsum('jsr,jsd->jrd', place[:, e], down.reshape(sources, CAP, chunk)...  11.8 us
    dot_general x8, matrix products, shards(): jnp.dot(hidden_list[e], specialist_contract_factor[0, e][:, c * chunk:(c...  11.2 us
    dot_general x4, matrix products, shards(): jnp.dot(rows_in, specialist_switch_factor[0, e], preferred_element_type=j...  10.9 us
    dot_general x2, matrix products, attend(): jnp.einsum('thl,kl->thk', q_lat, key_rows, preferred_element_type=jnp.flo...  9.03 us
  transfers between devices with their start and end apart: 7, of which 7 were waited for; matrix products, arithmetic and copies ran while one was open for 6% of the time, Pallas kernels for 0%

commit v1 on v0

--- a/solution.py
+++ b/solution.py
@@ -6,6 +6,27 @@
 CAP = 64
 RETURN_CHUNKS = 2
 epsilon = 1e-06
+
+
+def gather_around(x, axis, dim):
+    size, here, rows = (lax.axis_size(axis), lax.axis_index(axis), x.shape[dim])
+    right = [(i, (i + 1) % size) for i in range(size)]
+    left = [(i, (i - 1) % size) for i in range(size)]
+    result = jnp.zeros((*x.shape[:dim], size * rows, *x.shape[dim + 1 :]), x.dtype)
+    result = lax.dynamic_update_slice_in_dim(result, x, here * rows, axis=dim)
+    from_left = from_right = x
+    half = size // 2
+    for step in range(1, half + 1):
+        from_left = lax.ppermute(from_left, axis, right)
+        result = lax.dynamic_update_slice_in_dim(
+            result, from_left, (here - step) % size * rows, axis=dim
+        )
+        if step < size - half:
+            from_right = lax.ppermute(from_right, axis, left)
+            result = lax.dynamic_update_slice_in_dim(
+                result, from_right, (here + step) % size * rows, axis=dim
+            )
+    return result
 
 
 def shifted(value, axis, steps):
@@ -143,7 +164,7 @@
         whole_rows = lax.all_gather(moe_input, "tensor", axis=1, tiled=True)
         place = placed[step_index]
         share = slot_share[step_index]
-        all_rows = lax.all_gather(whole_rows, "expert", axis=0, tiled=True)
+        all_rows = gather_around(whole_rows, "expert", 0)
         all_rows = all_rows.reshape(sources, piece_list, full_width)
         hidden_list = []
         for e in range(expert_local):

time: 374 us -> 417 us (1.11)
  starting transfers between devices: 4.1 us -> 26.9 us
  local copies, waits for them, and re-layouts: 10.7 us -> 30.9 us
  waiting for transfers between devices: 212 us -> 205 us
  blocking collectives: 16.3 us -> 20.9 us
    all_gather x2 -> x0, waiting for transfers between devices: 73.9 us -> none  [shards(): all_rows = lax.all_gather(whole_rows, 'expert', axis=0, tiled=True)]
    ppermute x0 -> x14, waiting for transfers between devices: none -> 65 us  [the longest x8 64.9 us: gather_around(): from_left = lax.ppermute(from_left, axis, right)]
    ppermute x0 -> x14, starting transfers between devices: none -> 22.9 us  [the longest x6 21.3 us: gather_around(): from_right = lax.ppermute(from_right, axis, left)]
    dynamic_update_slice x0 -> x14, local copies, waits for them, and re-layouts: none -> 17.1 us  [the longest x8 8.83 us: gather_around(): lax.dynamic_update_slice_in_dim(result, from_left, (here - step) % size *...]
    another operation x0 -> x2, local copies, waits for them, and re-layouts: none -> 5.04 us
    dot_general x4, matrix products: 7.47 us -> 12.4 us  [shards(): jnp.einsum('jsr,jrd->jsd', place[:, e], all_rows, preferred_element_type=...]
    all_gather x1, blocking collectives: 16.3 us -> 20.9 us  [shards(): lax.all_gather(jnp.swapaxes(shares_dense, 1, 2), 'expert', axis=1, tiled=...]
  transfers between devices with their start and end apart: 7 -> 19, of which waited for: 7 -> 12; matrix products, arithmetic and copies ran while one was open for 6% -> 9% of each run, Pallas kernels for 0% -> 0%
where the time goes in v1:
time: 417 us; the launch traced here: 409 us
  waiting for transfers between devices  205 us (49%)
  matrix products  81.9 us (20%)
  local copies, waits for them, and re-layouts  30.9 us (7%)
  other arithmetic  29.3 us (7%)
  starting transfers between devices  26.9 us (6%)
  blocking collectives  20.9 us (5%)
  between operations  14.2 us (3%)
    reduce_scatter x4, waiting for transfers between devices, shards(): lax.psum_scatter(total, 'expert', scatter_dimension=0, tiled=True)  131 us
    ppermute x8, waiting for transfers between devices, gather_around(): from_left = lax.ppermute(from_left, axis, right)  64.9 us
    ppermute x6, starting transfers between devices, gather_around(): from_right = lax.ppermute(from_right, axis, left)  21.3 us
    all_gather x1, blocking collectives, shards(): lax.all_gather(jnp.swapaxes(shares_dense, 1, 2), 'expert', axis=1, tiled=...  20.9 us
    sub x2, other arithmetic, attend(): expd = jnp.where(visible[:, None, :], jnp.exp(scores - row_max), 0.0)  13.5 us
    dot_general x4, matrix products, shards(): jnp.einsum('jsr,jrd->jsd', place[:, e], all_rows, preferred_element_type=...  12.4 us
    dot_general x8, matrix products, shards(): jnp.einsum('jsr,jsd->jrd', place[:, e], down.reshape(sources, CAP, chunk)...  11.6 us
    dot_general x8, matrix products, shards(): jnp.dot(hidden_list[e], specialist_contract_factor[0, e][:, c * chunk:(c...  11.2 us
  transfers between devices with their start and end apart: 19, of which 12 were waited for; matrix products, arithmetic and copies ran while one was open for 9% of the time, Pallas kernels for 0%

profile of v1, /device:TPU:0, one launch (start us, length us, event | category | flops | bytes accessed | tf_op | source)
XLA Modules:
  0.0 408.9 jit_solution(3589690113084134344)
XLA Ops:
  20.2 4.5 %fusion.105 = f32[128,8,896]{2,0,1:T(8,128)} fusion(bf16[1,8,128,512]{3,2,1,0:T(8,128)(2,1)S(1)} %copy-done.5, bf16[128,512]{1,0:T(8,128)(2,1)S(1)} %multiply_convert_fusion.3, bf16[768,512]{1,0:T(8,128)(2,1)} %get-tuple-element.14, bf16[16,8,8,128]{3,2,1,0:T(8,128)(2,1)S(1)} %fusion.130), kind=kOutput, calls=%fused_computation.97 | convolution fusion | flops 1076101120 | bytes 5898240 | tf_op jit(solution)/shard_map/thl,kl->thk/dot_general | solution.py:49
  24.8 6.7 %fusion.191 = (f32[128,8]{0,1:T(8,128)S(1)}, f32[128,8,896]{2,0,1:T(8,128)}) fusion(f32[128,8,896]{2,0,1:T(8,128)} %fusion.105, pred[128,896]{1,0:T(8,128)(4,1)} %get-tuple-element.24), kind=kOutput, calls=%fused_computation.220 | output fusion | flops 6423423 | bytes 7458816 | tf_op jit(solution)/shard_map/sub | solution.py:56
  31.5 3.9 fusion.126
  42.8 4.0 collective-permute-start.1
  46.9 20.9 %all-gather = f32[2,128,128]{2,1,0:T(8,128)S(1)} all-gather(f32[2,16,128]{2,1,0:T(8,128)S(1)} %bitcast.301), channel_id=2, replica_groups=mesh['groups'=2,'expert'=8,'section'=2,'tensor'=1] {'expert'}, dimensions={1}, use_global_device_ids=true | all-gather | bytes 147456 | tf_op jit(solution)/shard_map/all_gather | solution.py:103
  67.8 6.2 %slice_bitcast_fusion = (bf16[704,2048]{1,0:T(8,128)(2,1)}, bf16[704,2048]{1,0:T(8,128)(2,1)}) fusion(bf16[1,2,704,2048]{3,2,1,0:T(8,128)(2,1)} %param.33), kind=kLoop, calls=%fused_computation.40 | loop fusion | bytes 11534336 | tf_op jit(solution)/shard_map/squeeze | solution.py:193
  78.8 11.8 %collective-permute-done.2 = bf16[128,2048]{1,0:T(8,128)(2,1)} collective-permute-done((bf16[128,2048]{1,0:T(8,128)(2,1)}, bf16[128,2048]{1,0:T(8,128)(2,1)}, u32[]{:S(2)}, u32[]{:S(2)}) %collective-permute-start.2) | collective-permute-done | bytes 524320 | tf_op jit(solution)/shard_map/ppermute | solution.py:20
  99.8 6.9 %collective-permute-done.4 = bf16[128,2048]{1,0:T(8,128)(2,1)S(1)} collective-permute-done((bf16[128,2048]{1,0:T(8,128)(2,1)}, bf16[128,2048]{1,0:T(8,128)(2,1)S(1)}, u32[]{:S(2)}, u32[]{:S(2)}) %collective-permute-start.4) | collective-permute-done | bytes 524320 | tf_op jit(solution)/shard_map/ppermute | solution.py:20
  110.8 6.8 %collective-permute-done.6 = bf16[128,2048]{1,0:T(8,128)(2,1)S(1)} collective-permute-done((bf16[128,2048]{1,0:T(8,128)(2,1)S(1)}, bf16[128,2048]{1,0:T(8,128)(2,1)S(1)}, u32[]{:S(2)}, u32[]{:S(2)}) %collective-permute-start.6) | collective-permute-done | bytes 524320 | tf_op jit(solution)/shard_map/ppermute | solution.py:20
  118.4 3.5 convolution_convert_fusion.2
  144.0 28.6 %reduce-scatter.5.cloned.1.call-done = bf16[128,1024]{1,0:T(8,128)(2,1)} async-done(((bf16[1024,1024]{1,0:T(8,128)(2,1)}), bf16[128,1024]{1,0:T(8,128)(2,1)}) %reduce-scatter.5.cloned.1.call-update) | async-done | bytes 262160 | tf_op jit(solution)/shard_map/reduce_scatter | solution.py:204
  172.7 36.8 %reduce-scatter.7.cloned.1.call-done = bf16[128,1024]{1,0:T(8,128)(2,1)} async-done(((bf16[1024,1024]{1,0:T(8,128)(2,1)}), bf16[128,1024]{1,0:T(8,128)(2,1)}) %reduce-scatter.7.cloned.1.call-update) | async-done | bytes 262160 | tf_op jit(solution)/shard_map/reduce_scatter | solution.py:204
  214.9 8.7 %collective-permute-done.7 = bf16[128,2048]{1,0:T(8,128)(2,1)S(1)} collective-permute-done((bf16[128,2048]{1,0:T(8,128)(2,1)}, bf16[128,2048]{1,0:T(8,128)(2,1)S(1)}, u32[]{:S(2)}, u32[]{:S(2)}) %collective-permute-start.7) | collective-permute-done | bytes 524320 | tf_op jit(solution)/shard_map/ppermute | solution.py:35
  228.8 4.8 %fusion.107 = f32[128,8,896]{2,0,1:T(8,128)} fusion(bf16[1,8,128,512]{3,2,1,0:T(8,128)(2,1)} %param.25, bf16[128,512]{1,0:T(8,128)(2,1)S(1)} %multiply_convert_fusion.2, bf16[768,512]{1,0:T(8,128)(2,1)} %get-tuple-element.13, bf16[16,8,8,128]{3,2,1,0:T(8,128)(2,1)S(1)} %fusion.127), kind=kOutput, calls=%fused_computation.99 | convolution fusion | flops 1076101120 | bytes 5898240 | tf_op jit(solution)/shard_map/thl,kl->thk/dot_general | solution.py:49
  233.6 6.8 %fusion.192 = (f32[128,8]{0,1:T(8,128)S(1)}, f32[128,8,896]{2,0,1:T(8,128)}) fusion(f32[128,8,896]{2,0,1:T(8,128)} %fusion.107, pred[128,896]{1,0:T(8,128)(4,1)S(1)} %copy-done.15), kind=kOutput, calls=%fused_computation.221 | output fusion | flops 6423423 | bytes 7458816 | tf_op jit(solution)/shard_map/sub | solution.py:56
  240.4 3.7 fusion.125
  250.6 3.5 collective-permute-start.9
  254.1 11.6 %collective-permute-done.8 = bf16[128,2048]{1,0:T(8,128)(2,1)S(1)} collective-permute-done((bf16[128,2048]{1,0:T(8,128)(2,1)S(1)}, bf16[128,2048]{1,0:T(8,128)(2,1)S(1)}, u32[]{:S(2)}, u32[]{:S(2)}) %collective-permute-start.8) | collective-permute-done | bytes 524320 | tf_op jit(solution)/shard_map/ppermute | solution.py:20
  265.7 3.5 collective-permute-start.11
  269.4 12.1 %collective-permute-done.10 = bf16[128,2048]{1,0:T(8,128)(2,1)S(1)} collective-permute-done((bf16[128,2048]{1,0:T(8,128)(2,1)S(1)}, bf16[128,2048]{1,0:T(8,128)(2,1)S(1)}, u32[]{:S(2)}, u32[]{:S(2)}) %collective-permute-start.10) | collective-permute-done | bytes 524320 | tf_op jit(solution)/shard_map/ppermute | solution.py:20
  288.5 8.0 %collective-permute-done.12 = bf16[128,2048]{1,0:T(8,128)(2,1)S(1)} collective-permute-done((bf16[128,2048]{1,0:T(8,128)(2,1)S(1)}, bf16[128,2048]{1,0:T(8,128)(2,1)S(1)}, u32[]{:S(2)}, u32[]{:S(2)}) %collective-permute-start.12) | collective-permute-done | bytes 524320 | tf_op jit(solution)/shard_map/ppermute | solution.py:20
  299.3 7.8 %collective-permute-done.14 = bf16[128,2048]{1,0:T(8,128)(2,1)S(1)} collective-permute-done((bf16[128,2048]{1,0:T(8,128)(2,1)S(1)}, bf16[128,2048]{1,0:T(8,128)(2,1)S(1)}, u32[]{:S(2)}, u32[]{:S(2)}) %collective-permute-start.14) | collective-permute-done | bytes 524320 | tf_op jit(solution)/shard_map/ppermute | solution.py:20
  333.3 28.6 %reduce-scatter.9.cloned.1.call-done = bf16[128,1024]{1,0:T(8,128)(2,1)} async-done(((bf16[1024,1024]{1,0:T(8,128)(2,1)}), bf16[128,1024]{1,0:T(8,128)(2,1)}) %reduce-scatter.9.cloned.1.call-update) | async-done | bytes 262160 | tf_op jit(solution)/shard_map/reduce_scatter | solution.py:204
  361.9 36.9 %reduce-scatter.11.cloned.1.call-done = bf16[128,1024]{1,0:T(8,128)(2,1)} async-done(((bf16[1024,1024]{1,0:T(8,128)(2,1)}), bf16[128,1024]{1,0:T(8,128)(2,1)}) %reduce-scatter.11.cloned.1.call-update) | async-done | bytes 262160 | tf_op jit(solution)/shard_map/reduce_scatter | solution.py:204
  (196 shorter events, 117.9 us)
Async XLA Ops:
  6.5 166.1 %reduce-scatter.5.cloned.1.call-start = ((), (), s32[]{:S(2)}) async-start(), calls=%async_computation.4 | async-start | bytes 2359296 | tf_op jit(solution)/shard_map/reduce_scatter | solution.py:204
  38.6 8.2 %copy-start.19 = (s32[2,1,128,6]{2,1,3,0:T(1,128)S(1)}, s32[2,1,128,6]{2,1,3,0:T(1,128)}, u32[]{:S(2)}) copy-start(s32[2,1,128,6]{2,1,3,0:T(1,128)} %param.21) | copy-start | bytes 18436
  38.6 8.2 %copy-start.20 = (f32[2,1,128,6]{2,1,3,0:T(1,128)S(1)}, f32[2,1,128,6]{2,1,3,0:T(1,128)}, u32[]{:S(2)}) copy-start(f32[2,1,128,6]{2,1,3,0:T(1,128)} %param.22) | copy-start | bytes 18436
  42.3 32.7 %collective-permute-start = (bf16[128,2048]{1,0:T(8,128)(2,1)}, bf16[128,2048]{1,0:T(8,128)(2,1)}, u32[]{:S(2)}, u32[]{:S(2)}) collective-permute-start(bf16[128,2048]{1,0:T(8,128)(2,1)} %get-tuple-element.10), channel_id=1, source_target_pairs={{0,2},{2,4},{4,6},{6,8},{8,10},{10,12},{12,14},{14,0},{1,3},{3,5},... | collective-permute-start | bytes 1572872 | tf_op jit(solution)/shard_map/ppermute | solution.py:20
  42.8 32.6 %collective-permute-start.1 = (bf16[128,2048]{1,0:T(8,128)(2,1)}, bf16[128,2048]{1,0:T(8,128)(2,1)}, u32[]{:S(2)}, u32[]{:S(2)}) collective-permute-start(bf16[128,2048]{1,0:T(8,128)(2,1)} %get-tuple-element.10), channel_id=1, source_target_pairs={{0,14},{2,0},{4,2},{6,4},{8,6},{10,8},{12,10},{14,12},{1,15},{3,1}... | collective-permute-start | bytes 1572872 | tf_op jit(solution)/shard_map/ppermute | solution.py:25
  75.0 15.7 %collective-permute-start.2 = (bf16[128,2048]{1,0:T(8,128)(2,1)}, bf16[128,2048]{1,0:T(8,128)(2,1)}, u32[]{:S(2)}, u32[]{:S(2)}) collective-permute-start(bf16[128,2048]{1,0:T(8,128)(2,1)} %collective-permute-done), channel_id=1, source_target_pairs={{0,2},{2,4},{4,6},{6,8},{8,10},{10,12},{12,14},{14,0},{1,3},{3,5},... | collective-permute-start | bytes 1572872 | tf_op jit(solution)/shard_map/ppermute | solution.py:20
  75.4 19.1 %collective-permute-start.3 = (bf16[128,2048]{1,0:T(8,128)(2,1)}, bf16[128,2048]{1,0:T(8,128)(2,1)}, u32[]{:S(2)}, u32[]{:S(2)}) collective-permute-start(bf16[128,2048]{1,0:T(8,128)(2,1)} %collective-permute-done.1), channel_id=1, source_target_pairs={{0,14},{2,0},{4,2},{6,4},{8,6},{10,8},{12,10},{14,12},{1,15},{3,1}... | collective-permute-start | bytes 1572872 | tf_op jit(solution)/shard_map/ppermute | solution.py:25
  90.6 16.0 %collective-permute-start.4 = (bf16[128,2048]{1,0:T(8,128)(2,1)}, bf16[128,2048]{1,0:T(8,128)(2,1)S(1)}, u32[]{:S(2)}, u32[]{:S(2)}) collective-permute-start(bf16[128,2048]{1,0:T(8,128)(2,1)} %collective-permute-done.2), channel_id=1, source_target_pairs={{0,2},{2,4},{4,6},{6,8},{8,10},{10,12},{12,14},{14,0},{1,3},{3,5},... | collective-permute-start | bytes 1572872 | tf_op jit(solution)/shard_map/ppermute | solution.py:20
  94.5 15.5 %collective-permute-start.5 = (bf16[128,2048]{1,0:T(8,128)(2,1)}, bf16[128,2048]{1,0:T(8,128)(2,1)S(1)}, u32[]{:S(2)}, u32[]{:S(2)}) collective-permute-start(bf16[128,2048]{1,0:T(8,128)(2,1)} %collective-permute-done.3), channel_id=1, source_target_pairs={{0,14},{2,0},{4,2},{6,4},{8,6},{10,8},{12,10},{14,12},{1,15},{3,1}... | collective-permute-start | bytes 1572872 | tf_op jit(solution)/shard_map/ppermute | solution.py:25
  106.7 10.9 %collective-permute-start.6 = (bf16[128,2048]{1,0:T(8,128)(2,1)S(1)}, bf16[128,2048]{1,0:T(8,128)(2,1)S(1)}, u32[]{:S(2)}, u32[]{:S(2)}) collective-permute-start(bf16[128,2048]{1,0:T(8,128)(2,1)S(1)} %collective-permute-done.4), channel_id=1, source_target_pairs={{0,2},{2,4},{4,6},{6,8},{8,10},{10,12},{12,14},{14,0},{1,3},{3,5},... | collective-permute-start | bytes 1572872 | tf_op jit(solution)/shard_map/ppermute | solution.py:20
  117.6 7.2 %slice-start = ((s8[5767168]{0:T(1024)(128)(4,1)}), s8[4194304]{0:T(1024)(128)(4,1)S(1)}, s32[]{:S(2)}) async-start(s8[5767168]{0:T(1024)(128)(4,1)} %bitcast.312), calls=%async_computation.8 | async-start | bytes 8388608
  137.1 72.4 %reduce-scatter.7.cloned.1.call-start = ((), (), s32[]{:S(2)}) async-start(), calls=%async_computation.5 | async-start | bytes 2359296 | tf_op jit(solution)/shard_map/reduce_scatter | solution.py:204
  144.0 217.9 %reduce-scatter.9.cloned.1.call-start = ((), (), s32[]{:S(2)}) async-start(), calls=%async_computation.6 | async-start | bytes 2359296 | tf_op jit(solution)/shard_map/reduce_scatter | solution.py:204
  211.4 12.1 %collective-permute-start.7 = (bf16[128,2048]{1,0:T(8,128)(2,1)}, bf16[128,2048]{1,0:T(8,128)(2,1)S(1)}, u32[]{:S(2)}, u32[]{:S(2)}) collective-permute-start(bf16[128,2048]{1,0:T(8,128)(2,1)} %add_convert_fusion.5), channel_id=1, source_target_pairs={{0,1},{2,3},{4,5},{6,7},{8,9},{10,11},{12,13},{14,15},{16,17},{18,... | collective-permute-start | bytes 1572872 | tf_op jit(solution)/shard_map/ppermute | solution.py:35
  250.6 15.1 %collective-permute-start.8 = (bf16[128,2048]{1,0:T(8,128)(2,1)S(1)}, bf16[128,2048]{1,0:T(8,128)(2,1)S(1)}, u32[]{:S(2)}, u32[]{:S(2)}) collective-permute-start(bf16[128,2048]{1,0:T(8,128)(2,1)S(1)} %get-tuple-element.6), channel_id=1, source_target_pairs={{0,2},{2,4},{4,6},{6,8},{8,10},{10,12},{12,14},{14,0},{1,3},{3,5},... | collective-permute-start | bytes 1572872 | tf_op jit(solution)/shard_map/ppermute | solution.py:20
  250.6 15.1 %collective-permute-start.9 = (bf16[128,2048]{1,0:T(8,128)(2,1)S(1)}, bf16[128,2048]{1,0:T(8,128)(2,1)}, u32[]{:S(2)}, u32[]{:S(2)}) collective-permute-start(bf16[128,2048]{1,0:T(8,128)(2,1)S(1)} %get-tuple-element.6), channel_id=1, source_target_pairs={{0,14},{2,0},{4,2},{6,4},{8,6},{10,8},{12,10},{14,12},{1,15},{3,1}... | collective-permute-start | bytes 1572872 | tf_op jit(solution)/shard_map/ppermute | solution.py:25
  265.7 15.8 %collective-permute-start.10 = (bf16[128,2048]{1,0:T(8,128)(2,1)S(1)}, bf16[128,2048]{1,0:T(8,128)(2,1)S(1)}, u32[]{:S(2)}, u32[]{:S(2)}) collective-permute-start(bf16[128,2048]{1,0:T(8,128)(2,1)S(1)} %collective-permute-done.8), channel_id=1, source_target_pairs={{0,2},{2,4},{4,6},{6,8},{8,10},{10,12},{12,14},{14,0},{1,3},{3,5},... | collective-permute-start | bytes 1572872 | tf_op jit(solution)/shard_map/ppermute | solution.py:20
  265.7 18.5 %collective-permute-start.11 = (bf16[128,2048]{1,0:T(8,128)(2,1)}, bf16[128,2048]{1,0:T(8,128)(2,1)S(1)}, u32[]{:S(2)}, u32[]{:S(2)}) collective-permute-start(bf16[128,2048]{1,0:T(8,128)(2,1)} %collective-permute-done.9), channel_id=1, source_target_pairs={{0,14},{2,0},{4,2},{6,4},{8,6},{10,8},{12,10},{14,12},{1,15},{3,1}... | collective-permute-start | bytes 1572872 | tf_op jit(solution)/shard_map/ppermute | solution.py:25
  281.5 15.1 %collective-permute-start.12 = (bf16[128,2048]{1,0:T(8,128)(2,1)S(1)}, bf16[128,2048]{1,0:T(8,128)(2,1)S(1)}, u32[]{:S(2)}, u32[]{:S(2)}) collective-permute-start(bf16[128,2048]{1,0:T(8,128)(2,1)S(1)} %collective-permute-done.10), channel_id=1, source_target_pairs={{0,2},{2,4},{4,6},{6,8},{8,10},{10,12},{12,14},{14,0},{1,3},{3,5},... | collective-permute-start | bytes 1572872 | tf_op jit(solution)/shard_map/ppermute | solution.py:20
  284.2 14.2 %collective-permute-start.13 = (bf16[128,2048]{1,0:T(8,128)(2,1)S(1)}, bf16[128,2048]{1,0:T(8,128)(2,1)S(1)}, u32[]{:S(2)}, u32[]{:S(2)}) collective-permute-start(bf16[128,2048]{1,0:T(8,128)(2,1)S(1)} %collective-permute-done.11), channel_id=1, source_target_pairs={{0,14},{2,0},{4,2},{6,4},{8,6},{10,8},{12,10},{14,12},{1,15},{3,1}... | collective-permute-start | bytes 1572872 | tf_op jit(solution)/shard_map/ppermute | solution.py:25
  296.5 10.6 %collective-permute-start.14 = (bf16[128,2048]{1,0:T(8,128)(2,1)S(1)}, bf16[128,2048]{1,0:T(8,128)(2,1)S(1)}, u32[]{:S(2)}, u32[]{:S(2)}) collective-permute-start(bf16[128,2048]{1,0:T(8,128)(2,1)S(1)} %collective-permute-done.12), channel_id=1, source_target_pairs={{0,2},{2,4},{4,6},{6,8},{8,10},{10,12},{12,14},{14,0},{1,3},{3,5},... | collective-permute-start | bytes 1572872 | tf_op jit(solution)/shard_map/ppermute | solution.py:20
  297.6 16.5 %slice-start.2 = ((s8[5767168]{0:T(1024)(128)(4,1)}), s8[4194304]{0:T(1024)(128)(4,1)S(1)}, s32[]{:S(2)}) async-start(s8[5767168]{0:T(1024)(128)(4,1)} %bitcast.314), calls=%async_computation.10 | async-start | bytes 8388608
  326.5 72.3 %reduce-scatter.11.cloned.1.call-start = ((), (), s32[]{:S(2)}) async-start(), calls=%async_computation.7 | async-start | bytes 2359296 | tf_op jit(solution)/shard_map/reduce_scatter | solution.py:204
  333.3 68.8 %copy-start.1 = (bf16[1,2048,512]{2,1,0:T(8,128)(2,1)S(1)}, bf16[1,2048,512]{2,1,0:T(8,128)(2,1)}, u32[]{:S(2)}) copy-start(bf16[1,2048,512]{2,1,0:T(8,128)(2,1)} %param.28) | copy-start | bytes 6291460
  (33 other events, 116.1 us)
Sparse Core Ops, SparseCore 0:
  137.2 35.4 reduce-scatter.4
  175.0 34.4 reduce-scatter.6
  326.6 35.2 reduce-scatter.8
  364.1 34.6 reduce-scatter.10
